TPU v7x, 256 devices: a whole 4x4x8 slice. The times are simulated.
256 devices in a mesh: row: 32 (over y, z_lo, core), col: 8 (over x, z_hi).
Axes of the slice: x: 4, y: 4, z: 8 (z_hi: 2, z_lo: 4; z = z_hi * 4 + z_lo), core: 2. Of those that a mesh axis runs over, the one named last changes fastest.
Arguments:
- features: bfloat16 [32768, 512], P(('row', 'col')), may hold values from -6 to 6
- edge_tiles: bfloat16 [8192, 128, 128], P(('row', 'col')), may hold values from 0 to 1
- tile_rows: int32 [256, 32], P(('row', 'col')), may hold values from 0 to 7
- tile_cols: int32 [256, 32], P(('row', 'col')), may hold values from 0 to 31
- tile_count: int32 [256], P(('row', 'col')), may hold values from 8 to 32, as said below
- node_order: int32 [256, 128], P(('row', 'col')), may hold values from 0 to 127, each once within a row
- w_self: bfloat16 [512, 512], replicated, may hold values from -0.25 to 0.25
- w_neigh: bfloat16 [512, 512], replicated, may hold values from -12 to 12
- bias_term: bfloat16 [512], replicated, may hold values from -3 to 3
- cotangent: bfloat16 [32768, 512], P(('row', 'col')), may hold values from -6 to 6
Outputs:
- activations: bfloat16 [32768, 512], P(('row', 'col'))
- feature_grad: float32 [32768, 512], P(('row', 'col'))
- self_grad: float32 [512, 512], replicated
- neigh_grad: float32 [512, 512], replicated
- bias_grad: float32 [512], replicated
Inputs may be any that keep to these rules, and one draw needn't show every extreme that they name: Only the first tile_count[b] slots of block b's tile list are valid; later slots are padding and are ignored. The busiest block holds 32 tiles and the lightest 32 // 4. `tile_rows`: tile coordinates may repeat within a block's list. `tile_cols`: tile coordinates may repeat within a block's list.
All inputs are finite; a program needn't handle non-finite values.
Results may differ from a plain program's by a relative error of at most 0.0042.
Values may be sent and summed in bfloat16 or wider, within the bound.
A program may use at most 64 MiB of HBM per device.

v0:
```python
import math
import jax
import jax.numpy as jnp
from jax import lax
from jax.sharding import PartitionSpec as P


def forward_tiles(edge_tiles, rows_at, cols_at, live_mask, column, row_tiles):
    tile_total, tile_size, _ = edge_tiles.shape
    channels = column.shape[1]
    col_blocks = column.reshape(-1, tile_size, channels)
    step_size = math.gcd(tile_total, 16)

    def forward_advance(step_index, carry):
        summed, degree = carry
        offset = step_index * step_size
        tile_group = lax.dynamic_slice_in_dim(edge_tiles, offset, step_size, 0)
        where_rows = lax.dynamic_slice_in_dim(rows_at, offset, step_size, 0)
        where_cols = lax.dynamic_slice_in_dim(cols_at, offset, step_size, 0)
        weights = lax.dynamic_slice_in_dim(live_mask, offset, step_size, 0)
        picked = col_blocks[where_cols]
        products = jnp.einsum(
            "tij,tjf->tif", tile_group, picked, preferred_element_type=jnp.float32
        )
        row_sums = jnp.sum(tile_group.astype(jnp.float32), axis=2)
        summed = summed.at[where_rows].add(products * weights[:, None, None])
        degree = degree.at[where_rows].add(row_sums * weights[:, None])
        return (summed, degree)

    start_sums = (
        jnp.zeros((row_tiles, tile_size, channels), jnp.float32),
        jnp.zeros((row_tiles, tile_size), jnp.float32),
    )
    return lax.fori_loop(0, tile_total // step_size, forward_advance, start_sums)


def backward_tiles(edge_tiles, rows_at, cols_at, live_mask, row_grads, col_tiles):
    tile_total, tile_size, _ = edge_tiles.shape
    channels = row_grads.shape[1]
    row_blocks = row_grads.reshape(-1, tile_size, channels)
    step_size = math.gcd(tile_total, 16)

    def backward_advance(step_index, summed):
        offset = step_index * step_size
        tile_group = lax.dynamic_slice_in_dim(edge_tiles, offset, step_size, 0)
        where_rows = lax.dynamic_slice_in_dim(rows_at, offset, step_size, 0)
        where_cols = lax.dynamic_slice_in_dim(cols_at, offset, step_size, 0)
        weights = lax.dynamic_slice_in_dim(live_mask, offset, step_size, 0)
        picked = row_blocks[where_rows]
        products = jnp.einsum(
            "tij,tif->tjf", tile_group, picked, preferred_element_type=jnp.float32
        )
        return summed.at[where_cols].add(products * weights[:, None, None])

    return lax.fori_loop(
        0,
        tile_total // step_size,
        backward_advance,
        jnp.zeros((col_tiles, tile_size, channels), jnp.float32),
    )


def times_transposed(left, right):
    return lax.dot_general(
        left, right, (((1,), (1,)), ((), ())), preferred_element_type=jnp.float32
    )


def shards(
    features,
    edge_tiles,
    tile_rows,
    tile_cols,
    tile_count,
    node_order,
    w_self,
    w_neigh,
    bias_term,
    cotangent,
):
    ordering = node_order[0]
    own_rows = features[ordering]
    node_dev = own_rows.shape[0]
    channels = own_rows.shape[1]
    tile_size = edge_tiles.shape[1]
    tile_total = edge_tiles.shape[0]
    col_count = lax.axis_size("col")
    row_count = lax.axis_size("row")
    live_mask = (jnp.arange(tile_total) < tile_count[0]).astype(jnp.float32)
    rows_at = tile_rows[0]
    cols_at = tile_cols[0]
    column = lax.all_gather(own_rows, "row", axis=0, tiled=True)
    summed, degree = forward_tiles(
        edge_tiles, rows_at, cols_at, live_mask, column, col_count * node_dev // tile_size
    )
    summed = summed.reshape(col_count * node_dev, channels)
    degree = degree.reshape(col_count * node_dev)
    own_sum, own_degree = (
        lax.psum_scatter(summed, "col", scatter_dimension=0, tiled=True),
        lax.psum_scatter(degree, "col", scatter_dimension=0, tiled=True),
    )
    inverse_degree = 1.0 / (1.0 + own_degree)
    neigh_mean = (own_sum * inverse_degree[:, None]).astype(jnp.bfloat16)
    preact = (
        jnp.dot(own_rows, w_self, preferred_element_type=jnp.float32)
        + jnp.dot(neigh_mean, w_neigh, preferred_element_type=jnp.float32)
        + bias_term.astype(jnp.float32)
    )
    activations = (jnp.maximum(preact, 0.0) + jnp.expm1(jnp.minimum(preact, 0.0))).astype(
        jnp.bfloat16
    )
    grad_pre = (cotangent.astype(jnp.float32) * jnp.exp(jnp.minimum(preact, 0.0))).astype(
        jnp.bfloat16
    )
    self_part = lax.dot_general(
        own_rows, grad_pre, (((0,), (0,)), ((), ())), preferred_element_type=jnp.float32
    )
    neigh_part = lax.dot_general(
        neigh_mean, grad_pre, (((0,), (0,)), ((), ())), preferred_element_type=jnp.float32
    )
    bias_part = jnp.sum(grad_pre.astype(jnp.float32), axis=0)
    self_grad, neigh_grad, bias_grad = lax.psum((self_part, neigh_part, bias_part), ("row", "col"))
    own_agg = (times_transposed(grad_pre, w_neigh) * inverse_degree[:, None]).astype(jnp.bfloat16)
    row_grads = lax.all_gather(own_agg, "col", axis=0, tiled=True)
    col_terms = backward_tiles(
        edge_tiles, rows_at, cols_at, live_mask, row_grads, row_count * node_dev // tile_size
    )
    own_grad = lax.psum_scatter(
        col_terms.reshape(row_count * node_dev, channels), "row", scatter_dimension=0, tiled=True
    )
    local_grad = times_transposed(grad_pre, w_self) + own_grad
    feature_grad = jnp.zeros_like(local_grad).at[ordering].set(local_grad)
    return (activations, feature_grad, self_grad, neigh_grad, bias_grad)


def solution(mesh):
    placed = (
        P(("row", "col"), None),
        P(("row", "col"), None, None),
        P(("row", "col"), None),
        P(("row", "col"), None),
        P(("row", "col")),
        P(("row", "col"), None),
        P(),
        P(),
        P(),
        P(("row", "col"), None),
    )
    return jax.shard_map(
        shards,
        mesh=mesh,
        in_specs=placed,
        out_specs=(P(("row", "col"), None), P(("row", "col"), None), P(), P(), P()),
        check_vma=False,
    )
```

profile of v0, /device:TPU:2, one launch (start us, length us, event | category | flops | bytes accessed | tf_op | source)
XLA Modules:
  0.0 742.1 jit_solution(8785978623316834144)
XLA Ops:
  7.2 0.7 fusion.11
  7.9 2.4 gather_fusion.2
  11.1 64.9 %all-gather.6.cloned.1.call-done = bf16[4096,512]{1,0:T(8,128)(2,1)} async-done(((bf16[128,512]{1,0:T(8,128)(2,1)}), bf16[4096,512]{1,0:T(8,128)(2,1)}) %all-gather.6.cloned.1.call-update) | async-done | bytes 4194320 | tf_op jit(solution)/shard_map/all_gather | solution.py:92
  76.0 0.2 broadcast_in_dim.52
  76.3 35.4 %while.28 = (s32[]{:T(128)}, f32[8,128,512]{2,1,0:T(8,128)S(1)}, f32[8,128]{1,0:T(8,128)S(1)}, s32[32]{0:T(128)}, bf16[32,128,128]{2,1,0:T(8,128)(2,1)}, /*index...) while((s32[]{:T(128)}, f32[8,128,512]{2,1,0:T(8,128)S(1)}, ...), condition=%wide.region_4.0_spmd, body=%wide.region_0.0_spmd.sunk | while | flops 271060064 | bytes 24143164 | solution.py:34
  76.4 0.8 compare_select_fusion.7
  77.2 4.3 gather_fusion
  81.4 0.1 dynamic_slice.75
  81.5 4.4 convolution_multiply_fusion.5
  85.9 6.1 scatter_fusion
  92.1 1.3 convert_reduce_fusion.3
  93.4 0.7 scatter_custom_fusion.12
  94.1 0.8 compare_select_fusion.7
  94.8 4.3 gather_fusion
  99.2 4.4 convolution_multiply_fusion.5
  103.6 6.1 scatter_fusion
  109.8 1.3 convert_reduce_fusion.3
  111.0 0.7 scatter_custom_fusion.12
  111.7 1.3 copy-done.1
  113.2 0.6 dynamic-slice
  114.5 0.2 fusion.14
  114.7 28.1 %all-reduce = f32[1024]{0:T(1024)S(1)} all-reduce(f32[1024]{0:T(1024)S(1)} %bitcast.36), channel_id=4, replica_groups=mesh['row'=32,'col'=8] {'col'}, use_global_device_ids=true, to_apply=%region_6.0.clone | all-reduce | flops 1024 | bytes 8192
  142.8 0.1 fusion.12
  142.9 65.3 %reduce-scatter.3.cloned.1.call-done = f32[128,512]{1,0:T(8,128)} async-done(((f32[1024,512]{1,0:T(8,128)}), f32[128,512]{1,0:T(8,128)}) %reduce-scatter.3.cloned.1.call-update) | async-done | bytes 262160 | tf_op jit(solution)/shard_map/reduce_scatter | solution.py:99
  208.2 2.0 convert_reduce_fusion.1
  210.2 1.0 fusion.8
  211.3 57.7 %all-gather.4.cloned.1.call-done = bf16[1024,512]{1,0:T(8,128)(2,1)} async-done(((bf16[128,512]{1,0:T(8,128)(2,1)}), bf16[1024,512]{1,0:T(8,128)(2,1)}) %all-gather.4.cloned.1.call-update) | async-done | bytes 1048592 | tf_op jit(solution)/shard_map/all_gather | solution.py:124
  269.0 4.3 broadcast_in_dim.54
  273.2 31.1 %while.29 = (s32[]{:T(128)}, f32[32,128,512]{2,1,0:T(8,128)}, s32[32]{0:T(128)S(1)}, bf16[32,128,128]{2,1,0:T(8,128)(2,1)}, s32[32]{0:T(128)S(1)}, /*index=5*/bf...) while((s32[]{:T(128)}, f32[32,128,512]{2,1,0:T(8,128)}, ...), condition=%wide.region_9.0_spmd, body=%wide.region_7.9_spmd.sunk | while | flops 270533728 | bytes 23597872 | solution.py:55
  273.2 0.1 compare_select_fusion.8
  273.3 1.9 gather_fusion.1
  275.2 0.1 dynamic_slice.78
  275.3 3.9 convolution_multiply_fusion.6
  279.2 9.6 %scatter_fusion.1 = f32[32,128,512]{2,1,0:T(8,128)} fusion(f32[32,128,512]{2,1,0:T(8,128)} %get-tuple-element.473, s32[16]{0:T(128)S(1)} %get-tuple-element.423, f32[16,128,512]{2,1,0:T(8,128)} %convolution_multiply_fusion.6), kind=kCustom, calls=%fused_computation.5.clone.1 | custom fusion | flops 1048576 | bytes 12582976 | tf_op jit(solution)/shard_map/while/body/eval_jaxpr/scatter-add | solution.py:53
  288.8 0.1 compare_select_fusion.8
  288.9 1.9 gather_fusion.1
  290.8 0.1 dynamic_slice.78
  290.9 3.9 convolution_multiply_fusion.6
  294.7 9.6 %scatter_fusion.1 = f32[32,128,512]{2,1,0:T(8,128)} fusion(f32[32,128,512]{2,1,0:T(8,128)} %get-tuple-element.473, s32[16]{0:T(128)S(1)} %get-tuple-element.423, f32[16,128,512]{2,1,0:T(8,128)} %convolution_multiply_fusion.6), kind=kCustom, calls=%fused_computation.5.clone.1 | custom fusion | flops 1048576 | bytes 12582976 | tf_op jit(solution)/shard_map/while/body/eval_jaxpr/scatter-add | solution.py:53
  304.4 1.3 fusion.15
  305.7 1.4 fusion.13
  307.1 74.2 %psum.23 = f32[512]{0:T(512)} all-reduce(f32[512]{0:T(512)S(1)} %get-tuple-element.318), channel_id=1, replica_groups=mesh['row'=32,'col'=8] {'row','col'}, use_global_device_ids=true, to_apply=%region_15.0 | all-reduce | flops 512 | bytes 4096 | tf_op jit(solution)/shard_map/psum | solution.py:122
  381.3 83.5 %reduce-scatter.5.cloned.1.call-done = f32[128,512]{1,0:T(8,128)} async-done(((f32[4096,512]{1,0:T(8,128)}), f32[128,512]{1,0:T(8,128)}) %reduce-scatter.5.cloned.1.call-update) | async-done | bytes 262160 | tf_op jit(solution)/shard_map/reduce_scatter | solution.py:128
  464.8 1.2 convolution_add_fusion
  466.0 1.7 scatter_custom_fusion.3
  467.7 263.4 %all-reduce.4.cloned.1.call-done = (f32[512,512]{1,0:T(8,128)}, f32[512,512]{1,0:T(8,128)}) async-done(((f32[512,512]{1,0:T(8,128)}, f32[512,512]{1,0:T(8,128)}), (f32[512,512]{1,0:T(8,128)}, f32[512,512]{1,0:T(8,128)})) %all-reduce.4.cloned.1.call-update) | async-done | bytes 2097168 | tf_op jit(solution)/shard_map/psum | solution.py:122
  731.1 2.3 copy.39
  733.4 2.3 copy.40
  (38 shorter events, 0.5 us)
Async XLA Ops:
  7.2 201.1 %copy-start = (bf16[512,512]{1,0:T(8,128)(2,1)S(1)}, bf16[512,512]{1,0:T(8,128)(2,1)}, u32[]{:S(2)}) copy-start(bf16[512,512]{1,0:T(8,128)(2,1)} %param.21) | copy-start | bytes 1572868
  7.2 68.8 %all-gather.6.cloned.1.call-start = ((), (), s32[]{:S(2)}) async-start(), calls=%async_computation.5 | async-start | bytes 4325376 | tf_op jit(solution)/shard_map/all_gather | solution.py:92
  10.4 197.8 %reduce-scatter.3.cloned.1.call-start = ((), (), s32[]{:S(2)}) async-start(), calls=%async_computation.2 | async-start | bytes 2359296 | tf_op jit(solution)/shard_map/reduce_scatter | solution.py:99
  76.3 36.9 %copy-start.8 = (bf16[512]{0:T(512)(128)(2,1)S(1)}, bf16[512]{0:T(512)(128)(2,1)}, u32[]{:S(2)}) copy-start(bf16[512]{0:T(512)(128)(2,1)} %param.22) | copy-start | bytes 3076
  76.3 36.9 %copy-start.9 = (u32[256]{0:T(256)S(1)}, u32[256]{0:T(256)}, u32[]{:S(2)}) copy-start(u32[256]{0:T(256)} %constant.100) | copy-start | bytes 3076
  76.3 38.1 %copy-start.2 = (bf16[128,512]{1,0:T(8,128)(2,1)S(1)}, bf16[128,512]{1,0:T(8,128)(2,1)}, u32[]{:S(2)}) copy-start(bf16[128,512]{1,0:T(8,128)(2,1)} %gather_fusion.2) | copy-start | bytes 393220
  76.3 38.1 %copy-start.3 = (bf16[512,512]{1,0:T(8,128)(2,1)S(1)}, bf16[512,512]{1,0:T(8,128)(2,1)}, u32[]{:S(2)}) copy-start(bf16[512,512]{1,0:T(8,128)(2,1)} %param.20) | copy-start | bytes 1572868
  76.3 131.9 %copy-start.5 = (bf16[128,512]{1,0:T(8,128)(2,1)S(1)}, bf16[128,512]{1,0:T(8,128)(2,1)}, u32[]{:S(2)}) copy-start(bf16[128,512]{1,0:T(8,128)(2,1)} %param.23) | copy-start | bytes 393220
  111.7 1.3 copy-start.1
  113.1 155.8 %all-gather.4.cloned.1.call-start = ((), (), s32[]{:S(2)}) async-start(), calls=%async_computation.3 | async-start | bytes 1179648 | tf_op jit(solution)/shard_map/all_gather | solution.py:124
  211.2 253.6 %reduce-scatter.5.cloned.1.call-start = ((), (), s32[]{:S(2)}) async-start(), calls=%async_computation.4 | async-start | bytes 8650752 | tf_op jit(solution)/shard_map/reduce_scatter | solution.py:128
  268.9 4.3 copy-start.6
  268.9 4.3 copy-start.7
  304.4 1.4 copy-start.4
  304.4 426.7 %all-reduce.4.cloned.1.call-start = ((), (), s32[]{:S(2)}) async-start(), calls=%async_computation.6 | async-start | bytes 4194304 | tf_op jit(solution)/shard_map/psum | solution.py:122
Sparse Core Ops, SparseCore 0:
  10.5 65.4 all-gather.5
  113.2 94.9 reduce-scatter.2
  211.4 57.4 all-gather.3
  304.5 160.2 reduce-scatter.4
  470.7 260.2 all-reduce.3
where the time goes:
time: 743 us; the launch traced here: 742 us
  waiting for transfers between devices  535 us (72%)
  blocking collectives  102 us (14%)
  other arithmetic  38 us (5%)
  local copies, waits for them, and re-layouts  27.8 us (4%)
  matrix products  23.6 us (3%)
  between operations  15.2 us (2%)
    psum x1, waiting for transfers between devices, shards(): lax.psum((self_part, neigh_part, bias_part), ('row', 'col'))  263 us
    reduce_scatter x1, waiting for transfers between devices, shards(): lax.psum_scatter(col_terms.reshape(row_count * node_dev, channels), 'row'...  83.5 us
    psum x1, blocking collectives, shards(): lax.psum((self_part, neigh_part, bias_part), ('row', 'col'))  74.2 us
    reduce_scatter x1, waiting for transfers between devices, shards(): lax.psum_scatter(summed, 'col', scatter_dimension=0, tiled=True)  65.3 us
    all_gather x1, waiting for transfers between devices, shards(): column = lax.all_gather(own_rows, 'row', axis=0, tiled=True)  64.9 us
    all_gather x1, waiting for transfers between devices, shards(): row_grads = lax.all_gather(own_agg, 'col', axis=0, tiled=True)  57.7 us
    unnamed x1, blocking collectives  28.1 us
    scatter-add x2, other arithmetic, backward_advance(): return summed.at[where_cols].add(products * weights[:, None, None])  19.3 us
  transfers between devices with their start and end apart: 5, of which 5 were waited for; matrix products, arithmetic and copies ran while one was open for 1% of the time, Pallas kernels for 0%

commit v1 on v0

--- a/solution.py
+++ b/solution.py
@@ -121,7 +121,10 @@
     bias_part = jnp.sum(grad_pre.astype(jnp.float32), axis=0)
     self_grad, neigh_grad, bias_grad = lax.psum((self_part, neigh_part, bias_part), ("row", "col"))
     own_agg = (times_transposed(grad_pre, w_neigh) * inverse_degree[:, None]).astype(jnp.bfloat16)
-    row_grads = lax.all_gather(own_agg, "col", axis=0, tiled=True)
+    passed = tuple((own_agg for _ in range(lax.axis_size("col"))))
+    local_next = jnp.stack(passed, 0)
+    all_values = lax.all_to_all(local_next, "col", 0, 0)
+    row_grads = jnp.concatenate(all_values, 0)
     col_terms = backward_tiles(
         edge_tiles, rows_at, cols_at, live_mask, row_grads, row_count * node_dev // tile_size
     )

time: 743 us -> 720 us (0.969)
  waiting for transfers between devices: 535 us -> 502 us
    all_gather x1 -> x0, waiting for transfers between devices: 57.7 us -> none  [shards(): row_grads = lax.all_gather(own_agg, 'col', axis=0, tiled=True)]
    all_to_all x0 -> x1, waiting for transfers between devices: none -> 26.4 us  [shards(): all_values = lax.all_to_all(local_next, 'col', 0, 0)]
where the time goes in v1:
time: 720 us; the launch traced here: 719 us
  waiting for transfers between devices  502 us (70%)
  blocking collectives  105 us (15%)
  other arithmetic  38 us (5%)
  local copies, waits for them, and re-layouts  30.6 us (4%)
  matrix products  22.9 us (3%)
  between operations  15.2 us (2%)
    psum x1, waiting for transfers between devices, shards(): lax.psum((self_part, neigh_part, bias_part), ('row', 'col'))  264 us
    reduce_scatter x1, waiting for transfers between devices, shards(): lax.psum_scatter(col_terms.reshape(row_count * node_dev, channels), 'row'...  80.7 us
    psum x1, blocking collectives, shards(): lax.psum((self_part, neigh_part, bias_part), ('row', 'col'))  77.2 us
    reduce_scatter x1, waiting for transfers between devices, shards(): lax.psum_scatter(summed, 'col', scatter_dimension=0, tiled=True)  65.3 us
    all_gather x1, waiting for transfers between devices, shards(): column = lax.all_gather(own_rows, 'row', axis=0, tiled=True)  64.9 us
    unnamed x1, blocking collectives  28.1 us
    all_to_all x1, waiting for transfers between devices, shards(): all_values = lax.all_to_all(local_next, 'col', 0, 0)  26.4 us
    scatter-add x2, other arithmetic, backward_advance(): return summed.at[where_cols].add(products * weights[:, None, None])  19.2 us
  transfers between devices with their start and end apart: 5, of which 5 were waited for; matrix products, arithmetic and copies ran while one was open for 1% of the time, Pallas kernels for 0%

profile of v1, /device:TPU:2, one launch (start us, length us, event | category | flops | bytes accessed | tf_op | source)
XLA Modules:
  0.0 718.7 jit_solution(7224226879735413189)
XLA Ops:
  7.2 0.7 fusion.11
  7.9 2.4 gather_fusion.2
  11.1 64.9 %all-gather.3.cloned.1.call-done = bf16[4096,512]{1,0:T(8,128)(2,1)} async-done(((bf16[128,512]{1,0:T(8,128)(2,1)}), bf16[4096,512]{1,0:T(8,128)(2,1)}) %all-gather.3.cloned.1.call-update) | async-done | bytes 4194320 | tf_op jit(solution)/shard_map/all_gather | solution.py:92
  76.0 0.2 broadcast_in_dim.52
  76.3 35.3 %while.28 = (s32[]{:T(128)}, f32[8,128,512]{2,1,0:T(8,128)S(1)}, f32[8,128]{1,0:T(8,128)S(1)}, s32[32]{0:T(128)}, bf16[32,128,128]{2,1,0:T(8,128)(2,1)}, /*index...) while((s32[]{:T(128)}, f32[8,128,512]{2,1,0:T(8,128)S(1)}, ...), condition=%wide.region_4.0_spmd, body=%wide.region_0.0_spmd.sunk | while | flops 271060064 | bytes 24143164 | solution.py:34
  76.4 0.8 compare_select_fusion.7
  77.2 4.2 gather_fusion
  81.5 4.4 convolution_multiply_fusion.5
  85.9 6.1 scatter_fusion
  92.1 1.3 convert_reduce_fusion.3
  93.3 0.7 scatter_custom_fusion.12
  94.1 0.8 compare_select_fusion.7
  94.8 4.2 gather_fusion
  99.1 4.4 convolution_multiply_fusion.5
  103.6 6.1 scatter_fusion
  109.7 1.3 convert_reduce_fusion.3
  111.0 0.7 scatter_custom_fusion.12
  111.7 1.3 copy-done.1
  113.1 0.6 dynamic-slice
  114.4 0.2 fusion.14
  114.6 28.1 %all-reduce = f32[1024]{0:T(1024)S(1)} all-reduce(f32[1024]{0:T(1024)S(1)} %bitcast.34), channel_id=4, replica_groups=mesh['row'=32,'col'=8] {'col'}, use_global_device_ids=true, to_apply=%region_6.0.clone | all-reduce | flops 1024 | bytes 8192
  142.7 0.1 fusion.12
  142.8 65.3 %reduce-scatter.3.cloned.1.call-done = f32[128,512]{1,0:T(8,128)} async-done(((f32[1024,512]{1,0:T(8,128)}), f32[128,512]{1,0:T(8,128)}) %reduce-scatter.3.cloned.1.call-update) | async-done | bytes 262160 | tf_op jit(solution)/shard_map/reduce_scatter | solution.py:99
  208.1 2.0 convert_reduce_fusion.1
  210.1 0.3 fusion.8
  210.4 1.1 stack.2
  211.4 4.5 all-to-all-start
  216.0 26.4 %all-to-all-done = bf16[8,128,512]{2,1,0:T(8,128)(2,1)S(1)} async-done(((bf16[8,128,512]{2,1,0:T(8,128)(2,1)}), bf16[8,128,512]{2,1,0:T(8,128)(2,1)S(1)}, u32[]{:S(2)}, u32[]{:S(2)}) %all-to-all-start) | async-done | bytes 1048608 | tf_op jit(solution)/shard_map/all_to_all | solution.py:126
  242.4 4.3 broadcast_in_dim.54
  246.7 32.8 %while.29 = (s32[]{:T(128)}, f32[32,128,512]{2,1,0:T(8,128)}, s32[32]{0:T(128)S(1)}, bf16[32,128,128]{2,1,0:T(8,128)(2,1)}, s32[32]{0:T(128)S(1)}, /*index=5*/bf...) while((s32[]{:T(128)}, f32[32,128,512]{2,1,0:T(8,128)}, ...), condition=%wide.region_9.0_spmd, body=%wide.region_7.9_spmd.sunk | while | flops 270533728 | bytes 31986536 | solution.py:55
  246.8 0.9 copy-done.2
  247.7 1.9 gather_fusion.1
  249.6 0.1 dynamic_slice.78
  249.7 3.8 convolution_multiply_fusion.6
  253.5 9.6 %scatter_fusion.1 = f32[32,128,512]{2,1,0:T(8,128)} fusion(f32[32,128,512]{2,1,0:T(8,128)} %get-tuple-element.473, s32[16]{0:T(128)S(1)} %get-tuple-element.423, f32[16,128,512]{2,1,0:T(8,128)} %convolution_multiply_fusion.6), kind=kCustom, calls=%fused_computation.5.clone.1 | custom fusion | flops 1048576 | bytes 12582976 | tf_op jit(solution)/shard_map/while/body/eval_jaxpr/scatter-add | solution.py:53
  263.2 0.9 copy-done.2
  264.1 1.9 gather_fusion.1
  266.1 3.8 convolution_multiply_fusion.6
  269.9 9.6 %scatter_fusion.1 = f32[32,128,512]{2,1,0:T(8,128)} fusion(f32[32,128,512]{2,1,0:T(8,128)} %get-tuple-element.473, s32[16]{0:T(128)S(1)} %get-tuple-element.423, f32[16,128,512]{2,1,0:T(8,128)} %convolution_multiply_fusion.6), kind=kCustom, calls=%fused_computation.5.clone.1 | custom fusion | flops 1048576 | bytes 12582976 | tf_op jit(solution)/shard_map/while/body/eval_jaxpr/scatter-add | solution.py:53
  279.6 1.3 fusion.15
  280.9 1.4 fusion.13
  282.3 77.2 %psum.23 = f32[512]{0:T(512)} all-reduce(f32[512]{0:T(512)S(1)} %get-tuple-element.318), channel_id=1, replica_groups=mesh['row'=32,'col'=8] {'row','col'}, use_global_device_ids=true, to_apply=%region_15.0 | all-reduce | flops 512 | bytes 4096 | tf_op jit(solution)/shard_map/psum | solution.py:122
  359.6 80.7 %reduce-scatter.5.cloned.1.call-done = f32[128,512]{1,0:T(8,128)} async-done(((f32[4096,512]{1,0:T(8,128)}), f32[128,512]{1,0:T(8,128)}) %reduce-scatter.5.cloned.1.call-update) | async-done | bytes 262160 | tf_op jit(solution)/shard_map/reduce_scatter | solution.py:131
  440.3 1.3 convolution_add_fusion
  441.5 1.7 scatter_custom_fusion.3
  443.2 264.4 %all-reduce.4.cloned.1.call-done = (f32[512,512]{1,0:T(8,128)}, f32[512,512]{1,0:T(8,128)}) async-done(((f32[512,512]{1,0:T(8,128)}, f32[512,512]{1,0:T(8,128)}), (f32[512,512]{1,0:T(8,128)}, f32[512,512]{1,0:T(8,128)})) %all-reduce.4.cloned.1.call-update) | async-done | bytes 2097168 | tf_op jit(solution)/shard_map/psum | solution.py:122
  707.7 2.3 copy.39
  709.9 2.3 copy.40
  (46 shorter events, 0.7 us)
Async XLA Ops:
  7.2 200.9 %copy-start = (bf16[512,512]{1,0:T(8,128)(2,1)S(1)}, bf16[512,512]{1,0:T(8,128)(2,1)}, u32[]{:S(2)}) copy-start(bf16[512,512]{1,0:T(8,128)(2,1)} %param.21) | copy-start | bytes 1572868
  7.2 68.8 %all-gather.3.cloned.1.call-start = ((), (), s32[]{:S(2)}) async-start(), calls=%async_computation.5 | async-start | bytes 4325376 | tf_op jit(solution)/shard_map/all_gather | solution.py:92
  10.4 197.6 %reduce-scatter.3.cloned.1.call-start = ((), (), s32[]{:S(2)}) async-start(), calls=%async_computation.3 | async-start | bytes 2359296 | tf_op jit(solution)/shard_map/reduce_scatter | solution.py:99
  76.3 36.8 %copy-start.10 = (bf16[512]{0:T(512)(128)(2,1)S(1)}, bf16[512]{0:T(512)(128)(2,1)}, u32[]{:S(2)}) copy-start(bf16[512]{0:T(512)(128)(2,1)} %param.22) | copy-start | bytes 3076
  76.3 36.8 %copy-start.11 = (u32[256]{0:T(256)S(1)}, u32[256]{0:T(256)}, u32[]{:S(2)}) copy-start(u32[256]{0:T(256)} %constant.100) | copy-start | bytes 3076
  76.3 38.0 %copy-start.4 = (bf16[128,512]{1,0:T(8,128)(2,1)S(1)}, bf16[128,512]{1,0:T(8,128)(2,1)}, u32[]{:S(2)}) copy-start(bf16[128,512]{1,0:T(8,128)(2,1)} %gather_fusion.2) | copy-start | bytes 393220
  76.3 38.0 %copy-start.5 = (bf16[512,512]{1,0:T(8,128)(2,1)S(1)}, bf16[512,512]{1,0:T(8,128)(2,1)}, u32[]{:S(2)}) copy-start(bf16[512,512]{1,0:T(8,128)(2,1)} %param.20) | copy-start | bytes 1572868
  76.3 131.7 %copy-start.7 = (bf16[128,512]{1,0:T(8,128)(2,1)S(1)}, bf16[128,512]{1,0:T(8,128)(2,1)}, u32[]{:S(2)}) copy-start(bf16[128,512]{1,0:T(8,128)(2,1)} %param.23) | copy-start | bytes 393220
  111.7 1.3 copy-start.1
  211.4 31.0 %all-to-all-start = ((bf16[8,128,512]{2,1,0:T(8,128)(2,1)}), bf16[8,128,512]{2,1,0:T(8,128)(2,1)S(1)}, u32[]{:S(2)}, u32[]{:S(2)}) async-start(bf16[8,128,512]{2,1,0:T(8,128)(2,1)} %stack.2), calls=%async_computation.1 | async-start | bytes 2097152 | tf_op jit(solution)/shard_map/all_to_all | solution.py:126
  216.0 224.3 %reduce-scatter.5.cloned.1.call-start = ((), (), s32[]{:S(2)}) async-start(), calls=%async_computation.4 | async-start | bytes 8650752 | tf_op jit(solution)/shard_map/reduce_scatter | solution.py:131
  216.0 30.7 %copy-start.8 = (s32[32]{0:T(128)S(1)}, s32[32]{0:T(128)}, u32[]{:S(2)}) copy-start(s32[32]{0:T(128)} %get-tuple-element.523) | copy-start | bytes 388
  216.0 30.7 %copy-start.9 = (s32[32]{0:T(128)S(1)}, s32[32]{0:T(128)}, u32[]{:S(2)}) copy-start(s32[32]{0:T(128)} %get-tuple-element.524) | copy-start | bytes 388
  246.7 1.0 copy-start.2
  253.5 9.6 %copy-start.3 = (bf16[8,128,512]{2,1,0:T(8,128)(2,1)S(1)}, bf16[8,128,512]{2,1,0:T(8,128)(2,1)}, u32[]{:S(2)}) copy-start(bf16[8,128,512]{2,1,0:T(8,128)(2,1)} %copy-done.2) | copy-start | bytes 3145732 | tf_op jit(solution)/shard_map/while
  263.1 1.0 copy-start.2
  269.9 9.6 %copy-start.3 = (bf16[8,128,512]{2,1,0:T(8,128)(2,1)S(1)}, bf16[8,128,512]{2,1,0:T(8,128)(2,1)}, u32[]{:S(2)}) copy-start(bf16[8,128,512]{2,1,0:T(8,128)(2,1)} %copy-done.2) | copy-start | bytes 3145732 | tf_op jit(solution)/shard_map/while
  279.6 1.4 copy-start.6
  279.6 428.1 %all-reduce.4.cloned.1.call-start = ((), (), s32[]{:S(2)}) async-start(), calls=%async_computation.6 | async-start | bytes 4194304 | tf_op jit(solution)/shard_map/psum | solution.py:122
Sparse Core Ops, SparseCore 0:
  10.5 65.4 all-gather.2
  113.2 94.8 reduce-scatter.2
  279.7 160.5 reduce-scatter.4
  446.3 261.3 all-reduce.3
